TPU v7x, 256 devices: a whole 4x4x8 slice. The times are simulated.
256 devices in a mesh: prow: 32 (over x, z), pcol: 8 (over y, core).
Axes of the slice: x: 4, y: 4, z: 8, core: 2. Of those that a mesh axis runs over, the one named last changes fastest.
Arguments:
- anc_inverse: bfloat16 [4, 32, 256, 16, 8, 256], P(None, 'prow', None, None, 'pcol'), may hold values from -6 to 6
- first_lower: bfloat16 [4, 32, 256, 256], P(None, 'prow', 'pcol'), may hold values from -0.046875 to 0.046875
- second_lower: bfloat16 [4, 32, 256, 256], P(None, 'prow', 'pcol'), may hold values from -0.0546875 to 0.0546875
- second_top: bfloat16 [256, 256], replicated, may hold values from -0.3125 to 0.3125
- struct_first: int32 [128], replicated, may hold values from 0 to 1
- struct_keep: int32 [128], replicated, may hold values from 0 to 1
- pivot_h: float32 [2, 256, 256], replicated, as said below
- pivot_s: float32 [2, 256, 256], replicated, as said below
- shifts: float32 [40], replicated, may hold values from 0.5 to 4
- pole_index: int32 [40], replicated, may hold values from 0 to 39, each once
Outputs:
- first_column: bfloat16 [4, 32, 256, 256], P(None, 'prow', 'pcol')
- first_diag: float32 [256, 256], replicated
- link_column: bfloat16 [256, 256], replicated
- second_column: bfloat16 [4, 32, 256, 256], P(None, 'prow', 'pcol')
- second_diag: float32 [256, 256], replicated
Inputs may be any that keep to these rules, and one draw needn't show every extreme that they name: `struct_first`: 1 marks a block row of the first supernode's structure. `struct_keep`: 1 marks a structure block that the second supernode keeps. `pole_index`: each pole appears once. `pivot_h`: symmetric, with a positive diagonal larger than each row's off-diagonal magnitudes together. `pivot_s`: symmetric, with a positive diagonal larger than each row's off-diagonal magnitudes together.
All inputs are finite; a program needn't handle non-finite values.
Results may differ from a plain program's by a relative error of at most 0.0041.
The roundings to bfloat16 on the way count: a program that leaves them out, or rounds other values in their place, can miss the bound.
Values may be sent and summed in bfloat16 or wider, within the bound.
A program may use at most 64 MiB of HBM per device.

v0:
```python
import jax
import jax.numpy as jnp
from jax import lax
from jax.sharding import PartitionSpec as P


def pivot_inverse(h_block, s_block, shift):
    factor = jnp.linalg.cholesky(h_block + shift * s_block)
    identity = jnp.eye(h_block.shape[0], dtype=jnp.float32)
    return jax.scipy.linalg.cho_solve((factor, True), identity)


def local_mask(flags, row_blocks, grid_rows, my_row):
    table = flags.reshape(row_blocks, grid_rows).astype(jnp.float32)
    return lax.dynamic_index_in_dim(table, my_row, axis=1, keepdims=False)


def per_device(
    anc_inverse,
    first_lower,
    second_lower,
    second_top,
    struct_first,
    struct_keep,
    pivot_h,
    pivot_s,
    shifts,
    pole_index,
):
    grid_rows = lax.axis_size("prow")
    grid_cols = lax.axis_size("pcol")
    my_row = lax.axis_index("prow")
    my_col = lax.axis_index("pcol")
    row_blocks = first_lower.shape[0]
    slab = first_lower.shape[2]
    width = first_lower.shape[3]
    col_blocks = anc_inverse.shape[3]
    first_mask = local_mask(struct_first, row_blocks, grid_rows, my_row)
    second_mask = first_mask * local_mask(struct_keep, row_blocks, grid_rows, my_row)
    lower_first = first_lower[:, 0] * first_mask.astype(jnp.bfloat16)[:, None, None]
    lower_second = second_lower[:, 0] * second_mask.astype(jnp.bfloat16)[:, None, None]
    stacked = jnp.concatenate([lower_first, lower_second], axis=2)[:, None]
    gathered = lax.all_gather(stacked, "prow", axis=1, tiled=True)
    grouped = gathered.reshape(row_blocks, grid_rows // grid_cols, grid_cols, slab, 2 * width)
    columns = lax.all_to_all(grouped, "pcol", split_axis=2, concat_axis=3, tiled=True)
    column_blocks = columns.reshape(col_blocks, width, 2 * width)
    inverse_rows = anc_inverse.reshape(row_blocks, width, col_blocks, width)
    totals = lax.psum(
        jnp.einsum(
            "axcy,cyz->xaz", inverse_rows, column_blocks, preferred_element_type=jnp.float32
        ),
        "pcol",
    )
    row_part = lax.dynamic_slice_in_dim(totals, my_col * slab, slab, 0)
    first_col = (-row_part[:, :, :width] * first_mask[None, :, None]).astype(jnp.bfloat16)
    bridge = jnp.einsum("raw,wz->raz", first_col, second_top, preferred_element_type=jnp.float32)
    second_col = (-(row_part[:, :, width:] + bridge) * second_mask[None, :, None]).astype(
        jnp.bfloat16
    )
    first_rows = lower_first.transpose(1, 0, 2)
    second_rows = lower_second.transpose(1, 0, 2)
    first_term = jnp.einsum(
        "ray,raz->yz", first_rows, first_col, preferred_element_type=jnp.float32
    )
    cross_term = jnp.einsum(
        "ray,raz->yz", first_col, second_rows, preferred_element_type=jnp.float32
    )
    second_term = jnp.einsum(
        "ray,raz->yz", second_rows, second_col, preferred_element_type=jnp.float32
    )
    first_sum, cross_sum, second_sum = lax.psum(
        (first_term, cross_term, second_term), ("prow", "pcol")
    )
    poles = jnp.arange(shifts.shape[0], dtype=jnp.int32)
    shift = jnp.sum(jnp.where(poles == pole_index[0], shifts, 0.0))
    first_diag = pivot_inverse(pivot_h[0], pivot_s[0], shift) - first_sum
    link_col = (
        -(
            cross_sum
            + jnp.dot(
                first_diag.astype(jnp.bfloat16), second_top, preferred_element_type=jnp.float32
            )
        )
    ).astype(jnp.bfloat16)
    second_diag = (
        pivot_inverse(pivot_h[1], pivot_s[1], shift)
        - second_sum
        - jnp.einsum("yz,yw->zw", second_top, link_col, preferred_element_type=jnp.float32)
    )
    return (
        first_col.transpose(1, 0, 2)[:, None],
        first_diag,
        link_col,
        second_col.transpose(1, 0, 2)[:, None],
        second_diag,
    )


def solution(mesh):
    return jax.shard_map(
        per_device,
        mesh=mesh,
        in_specs=(
            P(None, "prow", None, None, "pcol", None),
            P(None, "prow", "pcol", None),
            P(None, "prow", "pcol", None),
            P(),
            P(),
            P(),
            P(),
            P(),
            P(),
            P(),
        ),
        out_specs=(P(None, "prow", "pcol", None), P(), P(), P(None, "prow", "pcol", None), P()),
        check_vma=False,
    )
```

profile of v0, /device:TPU:8, one launch (start us, length us, event | category | flops | bytes accessed | tf_op | source)
XLA Modules:
  0.0 544.1 jit_solution(14048645056738182097)
XLA Ops:
  7.2 0.7 convert_element_type.47
  8.0 0.7 convert_element_type.44
  9.0 0.9 bitcast_multiply_fusion
  9.9 0.9 bitcast_multiply_fusion.1
  10.8 0.7 pad_maximum_fusion
  11.5 1.1 fusion.48
  12.7 1.1 fusion.47
  13.9 1.9 fusion.43
  15.8 0.7 fusion.23
  16.9 0.7 fusion.22
  17.7 0.7 fusion.11
  18.5 11.7 %cholesky.130 = f32[128,128]{1,0:T(8,128)S(1)} custom-call(f32[128,128]{1,0:T(8,128)S(1)} %cholesky.194), custom_call_target="Cholesky" | custom-call | tf_op jit(solution)/shard_map/jit(cholesky)/cholesky | solution.py:8
  30.3 9.8 %custom-call.15 = f32[1,128,128]{1,2,0:T(8,128)S(1)} custom-call(f32[1,128,128]{2,1,0:T(8,128)S(1)} %get-tuple-element.84), custom_call_target="InvertDiagBlocksLowerTriangular" | custom-call | tf_op jit(solution)/shard_map/jit(cholesky)/cholesky | solution.py:8
  40.6 11.7 %cholesky.147 = f32[128,128]{1,0:T(8,128)S(1)} custom-call(f32[128,128]{1,0:T(8,128)S(1)} %convolution_subtract_fusion.5), custom_call_target="Cholesky" | custom-call | tf_op jit(solution)/shard_map/jit(cholesky)/cholesky | solution.py:8
  52.3 0.6 compare_reduce_fusion.3
  53.0 0.6 compare_reduce_fusion.2
  55.0 41.5 %all-gather.3.cloned.1.call-done = bf16[4,1024,512]{2,1,0:T(8,128)(2,1)} async-done(((bf16[4,32,512]{2,1,0:T(8,128)(2,1)}), bf16[4,1024,512]{2,1,0:T(8,128)(2,1)}) %all-gather.3.cloned.1.call-update) | async-done | bytes 4194320 | tf_op jit(solution)/shard_map/all_gather | solution.py:43
  96.5 4.7 copy.82
  101.2 5.2 all-to-all-start
  106.4 4.0 while.4
  106.5 0.6 fusion.74
  107.0 1.4 bitcast_dynamic-update-slice_fusion.4
  108.5 0.6 fusion.74
  109.0 1.4 bitcast_dynamic-update-slice_fusion.4
  110.4 19.7 %custom-call.16 = f32[2,128,128]{1,2,0:T(8,128)S(1)} custom-call(f32[2,128,128]{2,1,0:T(8,128)S(1)} %get-tuple-element.21), custom_call_target="InvertDiagBlocksLowerTriangular" | custom-call | tf_op jit(solution)/shard_map/jit(_cho_solve)/triangular_solve | solution.py:10
  130.1 11.7 %cholesky.164 = f32[128,128]{1,0:T(8,128)S(1)} custom-call(f32[128,128]{1,0:T(8,128)S(1)} %cholesky.197), custom_call_target="Cholesky" | custom-call | tf_op jit(solution)/shard_map/jit(cholesky)/cholesky | solution.py:8
  141.9 9.8 %custom-call.17 = f32[1,128,128]{1,2,0:T(8,128)S(1)} custom-call(f32[1,128,128]{2,1,0:T(8,128)S(1)} %get-tuple-element.80), custom_call_target="InvertDiagBlocksLowerTriangular" | custom-call | tf_op jit(solution)/shard_map/jit(cholesky)/cholesky | solution.py:8
  152.2 11.7 %cholesky.181 = f32[128,128]{1,0:T(8,128)S(1)} custom-call(f32[128,128]{1,0:T(8,128)S(1)} %convolution_subtract_fusion.4), custom_call_target="Cholesky" | custom-call | tf_op jit(solution)/shard_map/jit(cholesky)/cholesky | solution.py:8
  163.9 0.6 compare_reduce_fusion.1
  164.6 0.6 compare_reduce_fusion
  166.6 4.0 while.5
  167.2 1.4 bitcast_dynamic-update-slice_fusion.5
  168.6 0.6 fusion.75
  169.2 1.4 bitcast_dynamic-update-slice_fusion.5
  170.6 19.9 %custom-call.18 = f32[2,128,128]{1,2,0:T(8,128)S(1)} custom-call(f32[2,128,128]{2,1,0:T(8,128)S(1)} %get-tuple-element.22), custom_call_target="InvertDiagBlocksLowerTriangular" | custom-call | tf_op jit(solution)/shard_map/jit(_cho_solve)/triangular_solve | solution.py:10
  192.3 2.5 copy.83
  194.8 9.6 %fusion.2 = f32[256,4,512]{2,0,1:T(8,128)} fusion(bf16[16,256,512,1]{2,1,0,3:T(8,128)(2,1)S(1)} %bitcast.134, bf16[4,256,16,256]{3,2,1,0:T(8,128)(2,1)} %bitcast.136), kind=kOutput, calls=%fused_computation.6 | convolution fusion | flops 4294967296 | bytes 14680064 | tf_op jit(solution)/shard_map/axcy,cyz->xaz/dot_general | solution.py:49
  206.0 64.4 %all-reduce.5.cloned.1.call-done = f32[256,4,512]{2,0,1:T(8,128)} async-done(((f32[256,4,512]{2,0,1:T(8,128)}), f32[256,4,512]{2,0,1:T(8,128)}) %all-reduce.5.cloned.1.call-update) | async-done | bytes 2097168 | tf_op jit(solution)/shard_map/psum | solution.py:48
  270.3 1.0 fusion.15
  271.3 0.9 convolution_bitcast_fusion.3
  272.2 0.9 convolution_bitcast_fusion.2
  273.1 1.1 fusion.10
  274.2 0.9 convolution_bitcast_fusion.1
  275.5 1.6 fusion.71
  277.1 256.3 %all-reduce.7.cloned.1.call-done = (f32[256,256]{1,0:T(8,128)}, f32[256,256]{1,0:T(8,128)}, f32[256,256]{1,0:T(8,128)}) async-done(((f32[256,256]{1,0:T(8,128)}, f32[256,256]{1,0:T(8,128)}, f32[256,256]{1,0:T(8,128)}), (f32[256,256]{1,0:T(8,128)}, f32[256,256]{1,0:T(8,128)}, f32[256,256]{1,0:T(8,128)})) %all-reduce.7.cloned.1.call-update) | async-done | bytes 786448 | tf_op jit(solution)/shard_map/psum | solution.py:71
  533.4 1.0 maximum_subtract_fusion
  534.4 1.2 fusion.7
  535.6 1.9 fusion.6
  (61 shorter events, 6.7 us)
Async XLA Ops:
  7.2 266.0 %copy-start = (bf16[256,256]{1,0:T(8,128)(2,1)S(1)}, bf16[256,256]{1,0:T(8,128)(2,1)}, u32[]{:S(2)}) copy-start(bf16[256,256]{1,0:T(8,128)(2,1)} %param.16) | copy-start | bytes 393220
  7.2 89.3 %all-gather.3.cloned.1.call-start = ((), (), s32[]{:S(2)}) async-start(), calls=%async_computation.2 | async-start | bytes 4325376 | tf_op jit(solution)/shard_map/all_gather | solution.py:43
  101.2 91.1 %all-to-all-start = ((bf16[4,4,8,32,512]{4,3,1,0,2:T(8,128)(2,1)}), bf16[4,4,8,32,512]{4,3,1,0,2:T(8,128)(2,1)}, u32[]{:S(2)}, u32[]{:S(2)}) async-start(bf16[4,4,8,32,512]{4,3,1,0,2:T(8,128)(2,1)} %copy.82), calls=%async_computation | async-start | bytes 8388608 | tf_op jit(solution)/shard_map/all_to_all | solution.py:45
  106.4 164.0 %all-reduce.5.cloned.1.call-start = ((), (), s32[]{:S(2)}) async-start(), calls=%async_computation.1 | async-start | bytes 4194304 | tf_op jit(solution)/shard_map/psum | solution.py:48
  204.4 329.0 %all-reduce.7.cloned.1.call-start = ((), (), s32[]{:S(2)}) async-start(), calls=%async_computation.3 | async-start | bytes 1572864 | tf_op jit(solution)/shard_map/psum | solution.py:71
  274.2 263.3 %copy-start.3 = (bf16[32,4,256]{2,0,1:T(8,128)(2,1)}, bf16[32,4,256]{2,0,1:T(8,128)(2,1)S(1)}, u32[]{:S(2)}) copy-start(bf16[32,4,256]{2,0,1:T(8,128)(2,1)S(1)} %fusion.10) | copy-start | bytes 196612
  534.4 3.2 copy-start.1
  535.6 2.0 copy-start.2
Sparse Core Ops, SparseCore 0:
  11.6 84.8 all-gather.2
  204.5 65.7 all-reduce.4
  276.7 256.6 all-reduce.6
where the time goes:
time: 545 us; the launch traced here: 544 us
  waiting for transfers between devices  362 us (66%)
  other arithmetic  120 us (22%)
  matrix products  20.9 us (4%)
  local copies, waits for them, and re-layouts  18.6 us (3%)
  between operations  16.7 us (3%)
    psum x1, waiting for transfers between devices, per_device(): lax.psum((first_term, cross_term, second_term), ('prow', 'pcol'))  256 us
    another operation x14, other arithmetic, pivot_inverse(): factor = jnp.linalg.cholesky(h_block + shift * s_block)  69.2 us
    psum x1, waiting for transfers between devices, per_device(): lax.psum(jnp.einsum('axcy,cyz->xaz', inverse_rows, column_blocks, preferr...  64.4 us
    all_gather x1, waiting for transfers between devices, per_device(): gathered = lax.all_gather(stacked, 'prow', axis=1, tiled=True)  41.5 us
    another operation x5, other arithmetic, pivot_inverse(): return jax.scipy.linalg.cho_solve((factor, True), identity)  39.6 us
  transfers between devices with their start and end apart: 4, of which 3 were waited for; matrix products, arithmetic and copies ran while one was open for 24% of the time, Pallas kernels for 0%

commit v1 on v0

--- a/solution.py
+++ b/solution.py
@@ -69,7 +69,7 @@
         "ray,raz->yz", second_rows, second_col, preferred_element_type=jnp.float32
     )
     first_sum, cross_sum, second_sum = lax.psum(
-        (first_term, cross_term, second_term), ("prow", "pcol")
+        lax.psum((first_term, cross_term, second_term), "pcol"), "prow"
     )
     poles = jnp.arange(shifts.shape[0], dtype=jnp.int32)
     shift = jnp.sum(jnp.where(poles == pole_index[0], shifts, 0.0))

time: 545 us -> 489 us (0.90)
  waiting for transfers between devices: 362 us -> 307 us
    psum x1 -> x2, waiting for transfers between devices: 256 us -> 218 us  [the longest x1 152 us: per_device(): lax.psum(lax.psum((first_term, cross_term, second_term), 'pcol'), 'prow')]
    psum x1, waiting for transfers between devices: 64.4 us -> 44.7 us  [per_device(): lax.psum(jnp.einsum('axcy,cyz->xaz', inverse_rows, column_blocks, preferr...]
  transfers between devices with their start and end apart: 4 -> 5, of which waited for: 3 -> 4; matrix products, arithmetic and copies ran while one was open for 24% -> 27% of each run, Pallas kernels for 0% -> 0%
where the time goes in v1:
time: 489 us; the launch traced here: 488 us
  waiting for transfers between devices  307 us (63%)
  other arithmetic  120 us (25%)
  matrix products  21.2 us (4%)
  local copies, waits for them, and re-layouts  18.6 us (4%)
  between operations  16.8 us (3%)
  starting transfers between devices  5.09 us (1%)
    psum x1, waiting for transfers between devices, per_device(): lax.psum(lax.psum((first_term, cross_term, second_term), 'pcol'), 'prow')  152 us
    another operation x14, other arithmetic, pivot_inverse(): factor = jnp.linalg.cholesky(h_block + shift * s_block)  69.2 us
    psum x1, waiting for transfers between devices, per_device(): lax.psum((first_term, cross_term, second_term), 'pcol')  66.2 us
    psum x1, waiting for transfers between devices, per_device(): lax.psum(jnp.einsum('axcy,cyz->xaz', inverse_rows, column_blocks, preferr...  44.7 us
    all_gather x1, waiting for transfers between devices, per_device(): gathered = lax.all_gather(stacked, 'prow', axis=1, tiled=True)  43.5 us
    another operation x5, other arithmetic, pivot_inverse(): return jax.scipy.linalg.cho_solve((factor, True), identity)  39.4 us
    dot_general x1, matrix products, per_device(): jnp.einsum('axcy,cyz->xaz', inverse_rows, column_blocks, preferred_elemen...  9.81 us
  transfers between devices with their start and end apart: 5, of which 4 were waited for; matrix products, arithmetic and copies ran while one was open for 27% of the time, Pallas kernels for 0%

profile of v1, /device:TPU:8, one launch (start us, length us, event | category | flops | bytes accessed | tf_op | source)
XLA Modules:
  0.0 488.3 jit_solution(17860784170273717539)
XLA Ops:
  7.2 0.7 convert_element_type.47
  8.0 0.7 convert_element_type.44
  9.0 0.9 bitcast_multiply_fusion
  9.9 0.9 bitcast_multiply_fusion.1
  10.8 0.7 pad_maximum_fusion
  11.5 1.1 fusion.48
  12.7 1.1 fusion.47
  13.9 1.9 fusion.43
  15.8 0.7 fusion.23
  16.9 0.7 fusion.22
  17.7 0.7 fusion.11
  18.5 11.7 %cholesky.130 = f32[128,128]{1,0:T(8,128)S(1)} custom-call(f32[128,128]{1,0:T(8,128)S(1)} %cholesky.194), custom_call_target="Cholesky" | custom-call | tf_op jit(solution)/shard_map/jit(cholesky)/cholesky | solution.py:8
  30.3 9.8 %custom-call.15 = f32[1,128,128]{1,2,0:T(8,128)S(1)} custom-call(f32[1,128,128]{2,1,0:T(8,128)S(1)} %get-tuple-element.87), custom_call_target="InvertDiagBlocksLowerTriangular" | custom-call | tf_op jit(solution)/shard_map/jit(cholesky)/cholesky | solution.py:8
  40.6 11.7 %cholesky.147 = f32[128,128]{1,0:T(8,128)S(1)} custom-call(f32[128,128]{1,0:T(8,128)S(1)} %convolution_subtract_fusion.5), custom_call_target="Cholesky" | custom-call | tf_op jit(solution)/shard_map/jit(cholesky)/cholesky | solution.py:8
  52.3 0.6 compare_reduce_fusion.3
  53.0 43.5 %all-gather.3.cloned.1.call-done = bf16[4,1024,512]{2,1,0:T(8,128)(2,1)} async-done(((bf16[4,32,512]{2,1,0:T(8,128)(2,1)}), bf16[4,1024,512]{2,1,0:T(8,128)(2,1)}) %all-gather.3.cloned.1.call-update) | async-done | bytes 4194320 | tf_op jit(solution)/shard_map/all_gather | solution.py:43
  96.5 4.7 copy.82
  101.2 5.0 %all-to-all-start = ((bf16[4,4,8,32,512]{4,3,1,0,2:T(8,128)(2,1)}), bf16[4,4,8,32,512]{4,3,1,0,2:T(8,128)(2,1)}, u32[]{:S(2)}, u32[]{:S(2)}) async-start(bf16[4,4,8,32,512]{4,3,1,0,2:T(8,128)(2,1)} %copy.82), calls=%async_computation | async-start | bytes 8388608 | tf_op jit(solution)/shard_map/all_to_all | solution.py:45
  106.2 0.6 compare_reduce_fusion.2
  108.2 4.0 while.4
  108.3 0.6 fusion.74
  108.8 1.4 bitcast_dynamic-update-slice_fusion.4
  110.9 1.4 bitcast_dynamic-update-slice_fusion.4
  112.2 19.7 %custom-call.16 = f32[2,128,128]{1,2,0:T(8,128)S(1)} custom-call(f32[2,128,128]{2,1,0:T(8,128)S(1)} %get-tuple-element.21), custom_call_target="InvertDiagBlocksLowerTriangular" | custom-call | tf_op jit(solution)/shard_map/jit(_cho_solve)/triangular_solve | solution.py:10
  131.9 11.7 %cholesky.164 = f32[128,128]{1,0:T(8,128)S(1)} custom-call(f32[128,128]{1,0:T(8,128)S(1)} %cholesky.197), custom_call_target="Cholesky" | custom-call | tf_op jit(solution)/shard_map/jit(cholesky)/cholesky | solution.py:8
  143.7 9.8 %custom-call.17 = f32[1,128,128]{1,2,0:T(8,128)S(1)} custom-call(f32[1,128,128]{2,1,0:T(8,128)S(1)} %get-tuple-element.83), custom_call_target="InvertDiagBlocksLowerTriangular" | custom-call | tf_op jit(solution)/shard_map/jit(cholesky)/cholesky | solution.py:8
  154.0 11.7 %cholesky.181 = f32[128,128]{1,0:T(8,128)S(1)} custom-call(f32[128,128]{1,0:T(8,128)S(1)} %convolution_subtract_fusion.4), custom_call_target="Cholesky" | custom-call | tf_op jit(solution)/shard_map/jit(cholesky)/cholesky | solution.py:8
  165.7 0.6 compare_reduce_fusion.1
  166.4 0.6 compare_reduce_fusion
  169.0 4.0 while.5
  169.6 1.4 bitcast_dynamic-update-slice_fusion.5
  171.0 0.6 fusion.75
  171.6 1.4 bitcast_dynamic-update-slice_fusion.5
  173.0 2.5 copy.83
  175.5 9.8 %fusion.2 = f32[256,4,512]{2,0,1:T(8,128)} fusion(bf16[16,256,512,1]{2,1,0,3:T(8,128)(2,1)S(1)} %bitcast.134, bf16[4,256,16,256]{3,2,1,0:T(8,128)(2,1)} %bitcast.136), kind=kOutput, calls=%fused_computation.6 | convolution fusion | flops 4294967296 | bytes 14680064 | tf_op jit(solution)/shard_map/axcy,cyz->xaz/dot_general | solution.py:49
  185.7 19.7 %custom-call.18 = f32[2,128,128]{1,2,0:T(8,128)S(1)} custom-call(f32[2,128,128]{2,1,0:T(8,128)S(1)} %get-tuple-element.22), custom_call_target="InvertDiagBlocksLowerTriangular" | custom-call | tf_op jit(solution)/shard_map/jit(_cho_solve)/triangular_solve | solution.py:10
  206.6 44.7 %all-reduce.7.cloned.1.call-done = f32[256,4,512]{2,0,1:T(8,128)} async-done(((f32[256,4,512]{2,0,1:T(8,128)}), f32[256,4,512]{2,0,1:T(8,128)}) %all-reduce.7.cloned.1.call-update) | async-done | bytes 2097168 | tf_op jit(solution)/shard_map/psum | solution.py:48
  251.3 1.0 fusion.15
  252.3 0.9 convolution_bitcast_fusion.3
  253.2 0.9 convolution_bitcast_fusion.2
  254.1 1.1 fusion.10
  255.2 0.9 convolution_bitcast_fusion.1
  256.8 66.2 %all-reduce.11.cloned.1.call-done = (f32[256,256]{1,0:T(8,128)}, f32[256,256]{1,0:T(8,128)}, f32[256,256]{1,0:T(8,128)}) async-done(((f32[256,256]{1,0:T(8,128)}, f32[256,256]{1,0:T(8,128)}, f32[256,256]{1,0:T(8,128)}), (f32[256,256]{1,0:T(8,128)}, f32[256,256]{1,0:T(8,128)}, f32[256,256]{1,0:T(8,128)})) %all-reduce.11.cloned.1.call-update) | async-done | bytes 786448 | tf_op jit(solution)/shard_map/psum | solution.py:72
  323.8 1.6 fusion.71
  325.5 152.1 %all-reduce.9.cloned.1.call-done = (f32[256,256]{1,0:T(8,128)}, f32[256,256]{1,0:T(8,128)}, f32[256,256]{1,0:T(8,128)}) async-done(((f32[256,256]{1,0:T(8,128)}, f32[256,256]{1,0:T(8,128)}, f32[256,256]{1,0:T(8,128)}), (f32[256,256]{1,0:T(8,128)}, f32[256,256]{1,0:T(8,128)}, f32[256,256]{1,0:T(8,128)})) %all-reduce.9.cloned.1.call-update) | async-done | bytes 786448 | tf_op jit(solution)/shard_map/psum | solution.py:71
  477.6 1.0 maximum_subtract_fusion
  478.6 1.2 fusion.7
  479.8 1.9 fusion.6
  (64 shorter events, 7.3 us)
Async XLA Ops:
  7.2 247.0 %copy-start = (bf16[256,256]{1,0:T(8,128)(2,1)S(1)}, bf16[256,256]{1,0:T(8,128)(2,1)}, u32[]{:S(2)}) copy-start(bf16[256,256]{1,0:T(8,128)(2,1)} %param.16) | copy-start | bytes 393220
  7.2 89.3 %all-gather.3.cloned.1.call-start = ((), (), s32[]{:S(2)}) async-start(), calls=%async_computation.2 | async-start | bytes 4325376 | tf_op jit(solution)/shard_map/all_gather | solution.py:43
  101.2 71.8 %all-to-all-start = ((bf16[4,4,8,32,512]{4,3,1,0,2:T(8,128)(2,1)}), bf16[4,4,8,32,512]{4,3,1,0,2:T(8,128)(2,1)}, u32[]{:S(2)}, u32[]{:S(2)}) async-start(bf16[4,4,8,32,512]{4,3,1,0,2:T(8,128)(2,1)} %copy.82), calls=%async_computation | async-start | bytes 8388608 | tf_op jit(solution)/shard_map/all_to_all | solution.py:45
  106.2 145.1 %all-reduce.7.cloned.1.call-start = ((), (), s32[]{:S(2)}) async-start(), calls=%async_computation.1 | async-start | bytes 4194304 | tf_op jit(solution)/shard_map/psum | solution.py:48
  185.4 137.6 %all-reduce.11.cloned.1.call-start = ((), (), s32[]{:S(2)}) async-start(), calls=%async_computation.4 | async-start | bytes 1572864 | tf_op jit(solution)/shard_map/psum | solution.py:72
  255.2 226.6 %copy-start.3 = (bf16[32,4,256]{2,0,1:T(8,128)(2,1)}, bf16[32,4,256]{2,0,1:T(8,128)(2,1)S(1)}, u32[]{:S(2)}) copy-start(bf16[32,4,256]{2,0,1:T(8,128)(2,1)S(1)} %fusion.10) | copy-start | bytes 196612
  256.2 221.4 %all-reduce.9.cloned.1.call-start = ((), (), s32[]{:S(2)}) async-start(), calls=%async_computation.3 | async-start | bytes 1572864 | tf_op jit(solution)/shard_map/psum | solution.py:71
  478.6 3.2 copy-start.1
  479.8 2.0 copy-start.2
Sparse Core Ops, SparseCore 0:
  11.6 84.8 all-gather.2
  185.5 65.7 all-reduce.6
  256.3 66.6 all-reduce.10
  327.0 150.5 all-reduce.8
